TPU v7x, 32 devices: a whole 2x2x4 slice. The times are simulated.
32 devices in a mesh: ma: 8 (over z, y), row: 4 (over x, core).
Axes of the slice: x: 2, y: 2, z: 4, core: 2. Of those that a mesh axis runs over, the one named last changes fastest.
Arguments:
- velocity: bfloat16 [3, 2, 16, 32, 65], P(None, None, 'row', 'ma'), may hold values from -6 to 6
- vorticity: bfloat16 [3, 2, 16, 32, 65], P(None, None, 'row', 'ma'), may hold values from -6 to 6
- legendre: bfloat16 [32, 65, 384], P('ma'), may hold values from -0.75 to 0.75
- pair_order: int32 [32], P('ma'), may hold values from 0 to 31, each once
- lat_weight: float32 [384], replicated, may hold values from 0.5 to 2
- diffusivity: float32 [16], replicated, may hold values from 0.25 to 2.5
Outputs:
- new_velocity: float32 [3, 2, 16, 32, 65], P(None, None, 'row', 'ma')
Inputs may be any that keep to these rules, and one draw needn't show every extreme that they name: pair_order holds each of 0 to 31 exactly once.
All inputs are finite; a program needn't handle non-finite values.
Results may differ from a plain program's by a relative error of at most 0.0095.
Values may be sent and summed in bfloat16 or wider, within the bound.
A program may use at most 128 MiB of HBM per device.

v0:
```python
import math
import jax
import jax.numpy as jnp
from jax import lax
from jax.sharding import PartitionSpec as P

NLON = 2048
STEP_SIZE = 1.0


def with_halo(cells, sides, width):
    for axis, dim in sides:
        count = lax.axis_size(axis)
        ends = count - 1
        head = lax.slice_in_dim(cells, 0, width, axis=dim)
        tail = lax.slice_in_dim(cells, cells.shape[dim] - width, cells.shape[dim], axis=dim)
        cells = jnp.concatenate(
            [
                lax.ppermute(tail, axis, [(i, (i + 1) % count) for i in range(ends)]),
                cells,
                lax.ppermute(head, axis, [((i + 1) % count, i) for i in range(ends)]),
            ],
            axis=dim,
        )
    return cells


def row_masks(low_order, pack_rows):
    orders_all = pack_rows - 1
    row_index = jnp.arange(pack_rows, dtype=jnp.int32)[None, :]
    low_column = low_order[:, None]
    is_lower = row_index < orders_all - low_column
    not_lower = jnp.logical_not(is_lower)
    even_low = row_index % 2 == 0
    even_high = (row_index + low_column) % 2 == 0
    low_pair = jnp.stack([is_lower & even_low, is_lower & jnp.logical_not(even_low)])
    high_pair = jnp.stack([not_lower & even_high, not_lower & jnp.logical_not(even_high)])
    return jnp.stack([low_pair, high_pair])


def cross_product(velocity_grid, vorticity_grid):
    return jnp.stack(
        [
            velocity_grid[1] * vorticity_grid[2] - velocity_grid[2] * vorticity_grid[1],
            velocity_grid[2] * vorticity_grid[0] - velocity_grid[0] * vorticity_grid[2],
            velocity_grid[0] * vorticity_grid[1] - velocity_grid[1] * vorticity_grid[0],
        ]
    )


def lon_table(column_order, is_imag, lon_start, lon_count):
    lon_index = lon_start + jnp.arange(lon_count, dtype=jnp.int32)
    angle_index = column_order[:, None] * lon_index[None, :] % NLON
    angle_value = angle_index.astype(jnp.float32) * (2.0 * math.pi / NLON)
    return jnp.where(is_imag[:, None], -jnp.sin(angle_value), jnp.cos(angle_value))


def local(velocity, vorticity, legendre, pair_order, lat_weight, diffusivity):
    pair_count = pair_order.shape[0]
    pack_rows = legendre.shape[1]
    half_lat = legendre.shape[2]
    nlat_all = 2 * half_lat
    levels_dev = velocity.shape[2]
    orders_all = pack_rows - 1
    inv_orders = 1.0 / math.sqrt(orders_all)
    inv_lon = 1.0 / math.sqrt(NLON)
    lon_width = NLON // 4
    mask_bool = row_masks(pair_order, pack_rows)
    fields = jnp.concatenate([velocity, vorticity], axis=0)
    masked = fields[None, None] * mask_bool.astype(jnp.bfloat16)[:, :, None, None, None]
    halves = jnp.einsum(
        "oqfilsr,srj->qfliosj", masked, legendre, preferred_element_type=jnp.float32
    )
    north_part = halves[0] + halves[1]
    south_part = halves[0] - halves[1]
    both_parts = jnp.concatenate([north_part, south_part], axis=-1)
    spectral = jnp.transpose(both_parts, (0, 1, 5, 2, 3, 4))
    spectral = spectral.reshape(6, levels_dev, nlat_all, 4 * pair_count).astype(jnp.bfloat16)
    gathered_ids = lax.all_gather(pair_order, "ma", axis=0, tiled=True)
    pair_slots = gathered_ids.reshape(-1, 1, 1, pair_count)
    both_orders = jnp.concatenate([pair_slots, orders_all - 1 - pair_slots], axis=2)
    full_shape = (both_orders.shape[0], 2, 2, pair_count)
    column_order = jnp.broadcast_to(both_orders, full_shape).reshape(-1)
    part_index = jnp.arange(2, dtype=jnp.int32)[None, :, None, None]
    is_imag = jnp.broadcast_to(part_index, full_shape).reshape(-1) == 1
    tables = [
        lon_table(column_order, is_imag, lon_block * lon_width, lon_width).astype(jnp.bfloat16)
        for lon_block in range(4)
    ]
    spec_block = lax.all_to_all(spectral, "ma", split_axis=2, concat_axis=3, tiled=True)
    accumulated = jnp.zeros((3,) + spec_block.shape[1:], jnp.float32)
    for lon_block in range(4):
        table_block = tables[lon_block]
        grid_values = (
            jnp.einsum("flac,cb->flab", spec_block, table_block, preferred_element_type=jnp.float32)
            * inv_orders
        )
        lamb_vector = cross_product(grid_values[:3], grid_values[3:])
        accumulated = accumulated + jnp.einsum(
            "flab,cb->flac",
            lamb_vector,
            table_block.astype(jnp.float32),
            precision=lax.Precision.HIGH,
            preferred_element_type=jnp.float32,
        )
    lamb_spec = (accumulated * inv_lon).astype(jnp.bfloat16)
    selector = jnp.transpose(mask_bool.astype(jnp.float32), (1, 0, 2, 3))[:, None, None, None]
    lamb_block = lax.all_to_all(lamb_spec, "ma", split_axis=3, concat_axis=2, tiled=True)
    item_count = lamb_block.shape[0]
    shaped = lamb_block.astype(jnp.float32).reshape(
        item_count, levels_dev, nlat_all, 2, 2, pair_count
    )
    shaped = jnp.transpose(shaped, (0, 1, 3, 4, 5, 2))
    north_side = shaped[..., :half_lat]
    south_side = shaped[..., half_lat:]
    weighted = jnp.stack(
        [lat_weight * (north_side + south_side), lat_weight * (north_side - south_side)]
    )
    weighted = weighted.astype(jnp.bfloat16)
    projected = jnp.einsum(
        "qfliosj,srj->qfliosr", weighted, legendre, preferred_element_type=jnp.float32
    )
    picked = jnp.sum(projected * selector, axis=(0, 4))
    tendency = jnp.transpose(picked, (0, 2, 1, 3, 4))
    source = velocity.astype(jnp.float32) + STEP_SIZE * tendency
    row_start = lax.axis_index("row") * levels_dev
    level_total = levels_dev * lax.axis_size("row")
    extended = with_halo(source.astype(jnp.bfloat16), (("row", 2),), 2).astype(source.dtype)
    padded_coupling = jnp.pad(diffusivity, (2, 2))
    wide_coupling = lax.dynamic_slice_in_dim(padded_coupling, row_start, levels_dev + 4)[
        None, None, :, None, None
    ]
    inner_coupling = wide_coupling[:, :, 1:-1]
    first_wide = (
        extended[:, :, 1:-1] + inner_coupling * (extended[:, :, :-2] + extended[:, :, 2:])
    ) / (1.0 + 2.0 * inner_coupling)
    global_level = row_start - 1 + jnp.arange(levels_dev + 2, dtype=jnp.int32)
    inside = ((global_level >= 0) & (global_level < level_total)).astype(jnp.float32)
    first_wide = first_wide * inside[None, None, :, None, None]
    own_coupling = wide_coupling[:, :, 2:-2]
    return (source + own_coupling * (first_wide[:, :, :-2] + first_wide[:, :, 2:])) / (
        1.0 + 2.0 * own_coupling
    )


def solution(mesh):
    in_specs = (
        P(None, None, "row", "ma", None),
        P(None, None, "row", "ma", None),
        P("ma", None, None),
        P("ma"),
        P(),
        P(),
    )
    out_specs = P(None, None, "row", "ma", None)
    return jax.shard_map(local, mesh=mesh, in_specs=in_specs, out_specs=out_specs, check_vma=False)
```

profile of v0, /device:TPU:1, one launch (start us, length us, event | category | flops | bytes accessed | tf_op | source)
XLA Modules:
  0.0 95.0 jit_solution(11931700865630016753)
XLA Ops:
  0.0 0.0 copy-start
  0.0 0.7 broadcast_subtract_fusion.1
  0.7 0.7 fusion.112
  1.5 0.8 pad_maximum_fusion
  2.3 0.0 copy-done
  2.3 0.3 convolution_bitcast_fusion
  2.7 0.1 fusion.42
  2.8 0.1 fusion.43
  2.9 0.2 maximum_bitcast_fusion
  3.0 0.2 copy.71
  3.3 5.8 %copy.72 = bf16[6,4,768,16]{3,1,0,2:T(4,128)(2,1)} copy(bf16[6,4,768,16]{2,1,3,0:T(4,128)(2,1)S(1)} %bitcast.115) | data formatting | bytes 1179648 | tf_op jit(solution)/shard_map/convert_element_type | solution.py:78
  9.1 0.0 copy-start.5
  9.1 7.0 %reshape.343 = bf16[8,2,18432]{2,1,0:T(2,128)(2,1)} reshape(bf16[768,6,4,16]{3,2,1,0:T(4,128)(2,1)} %bitcast.112) | data formatting | bytes 1179648
  16.1 6.4 %all-to-all-start = ((bf16[8,2,18432]{2,1,0:T(2,128)(2,1)}), bf16[8,2,18432]{2,1,0:T(2,128)(2,1)S(1)}, u32[]{:S(2)}, u32[]{:S(2)}) async-start(bf16[8,2,18432]{2,1,0:T(2,128)(2,1)} %reshape.343), calls=%async_computation | async-start | bytes 1179648 | tf_op jit(solution)/shard_map/all_to_all | solution.py:90
  22.4 0.0 copy-done.5
  22.4 0.6 dynamic-slice
  23.7 0.0 copy-done.3
  23.7 0.2 dynamic-update-slice
  23.9 13.4 %all-reduce.1 = s32[32]{0:T(128)S(1)} all-reduce(s32[32]{0:T(128)S(1)} %dynamic-update-slice), channel_id=1, replica_groups=mesh['ma'=8,'row'=4] {'ma'}, use_global_device_ids=true, to_apply=%add.1 | all-reduce | flops 32 | bytes 256
  37.3 0.1 reshape.329
  37.5 0.1 mul.250
  37.6 0.1 eq.67
  37.8 0.0 all-to-all-done
  37.8 4.4 %reshape.344 = bf16[768,6,4,16]{3,2,1,0:T(4,128)(2,1)} reshape(bf16[8,2,18432]{2,1,0:T(2,128)(2,1)S(1)} %all-to-all-done) | data formatting | bytes 1179648
  42.2 6.0 %copy.102 = bf16[6,4,8,96,16]{3,4,2,1,0:T(8,128)(2,1)S(1)} copy(bf16[6,4,8,96,16]{4,1,0,3,2:T(4,128)(2,1)} %bitcast.113) | data formatting | bytes 1179648 | tf_op jit(solution)/shard_map/all_to_all | solution.py:90
  48.2 1.9 %broadcast_multiply_fusion.3 = f32[6,4,96,512]{3,2,1,0:T(8,128)S(1)} fusion(bf16[6,4,96,128]{2,3,1,0:T(8,128)(2,1)S(1)} %bitcast.108, s32[128]{0:T(128)S(1)} %mul.250, pred[128]{0:T(512)(128)(4,1)S(1)} %eq.67), kind=kOutput, calls=%fused_computation.27 | convolution fusion | flops 304283648 | bytes 5309056 | tf_op jit(solution)/shard_map/flac,cb->flab/dot_general | solution.py:95
  50.1 0.6 multiply_subtract_fusion.11
  50.7 1.9 %broadcast_multiply_fusion.2 = f32[6,4,96,512]{3,2,1,0:T(8,128)S(1)} fusion(bf16[6,4,96,128]{2,3,1,0:T(8,128)(2,1)S(1)} %bitcast.109, s32[512]{0:T(512)S(1)} %iota_add_fusion.2, s32[128]{0:T(128)S(1)} %mul.250, pred[128]{0:T(512)(128)(4,1)S(1)} %eq.67), kind=kOutput, calls=%fused_computation.26 | convolution fusion | flops 304283648 | bytes 5311104 | tf_op jit(solution)/shard_map/flac,cb->flab/dot_general | solution.py:95
  52.5 0.6 multiply_subtract_fusion.8
  53.1 1.9 %broadcast_multiply_fusion.1 = f32[6,4,96,512]{3,2,1,0:T(8,128)S(1)} fusion(bf16[6,4,96,128]{2,3,1,0:T(8,128)(2,1)S(1)} %bitcast.110, s32[512]{0:T(512)S(1)} %iota_add_fusion.1, s32[128]{0:T(128)S(1)} %mul.250, pred[128]{0:T(512)(128)(4,1)S(1)} %eq.67), kind=kOutput, calls=%fused_computation.25 | convolution fusion | flops 304283648 | bytes 5311104 | tf_op jit(solution)/shard_map/flac,cb->flab/dot_general | solution.py:95
  55.0 0.6 multiply_subtract_fusion.5
  55.5 1.9 %broadcast_multiply_fusion = f32[6,4,96,512]{3,2,1,0:T(8,128)S(1)} fusion(bf16[6,4,96,128]{2,3,1,0:T(8,128)(2,1)S(1)} %bitcast.111, s32[512]{0:T(512)S(1)} %iota_add_fusion, s32[128]{0:T(128)S(1)} %mul.250, pred[128]{0:T(512)(128)(4,1)S(1)} %eq.67), kind=kOutput, calls=%fused_computation.24 | convolution fusion | flops 304283648 | bytes 5311104 | tf_op jit(solution)/shard_map/flac,cb->flab/dot_general | solution.py:95
  57.4 0.6 multiply_subtract_fusion.2
  58.0 1.8 %fusion = f32[3,4,96,128]{3,2,1,0:T(8,128)S(1)} fusion(f32[1,4,96,512]{3,2,1,0:T(8,128)S(1)} %get-tuple-element.16, f32[1,4,96,512]{3,2,1,0:T(8,128)S(1)} %get-tuple-element.15, f32[1,4,96,512]{3,2,1,0:T(8,128)S(1)} %get-tuple-element.14, s32[128]{0:T(128)S(1)} %mul.250, pred[128]{0:T(512)(128)(4,1)S(1)} %eq.67), kind=kOutput, calls=%fused_computation | convolution fusion | flops 455278592 | bytes 2949760 | tf_op jit(solution)/shard_map/flab,cb->flac/dot_general | solution.py:99
  59.8 2.1 %fusion.30 = f32[3,4,96,128]{3,2,1,0:T(8,128)S(1)} fusion(f32[3,4,96,128]{3,2,1,0:T(8,128)S(1)} %fusion, f32[1,4,96,512]{3,2,1,0:T(8,128)S(1)} %get-tuple-element.13, f32[1,4,96,512]{3,2,1,0:T(8,128)S(1)} %get-tuple-element.12, f32[1,4,96,512]{3,2,1,0:T(8,128)S(1)} %get-tuple-element.11, s32[512]{0:T(512)S(1)} %iota_add_fusion.2, s32[128]{0:T(128)S(1)} %mul.250, ...), kind=kOutput, calls=%fused_computation.31 | convolution fusion | flops 455426048 | bytes 3541632 | tf_op jit(solution)/shard_map/flab,cb->flac/dot_general | solution.py:99
  61.9 1.9 %fusion.27 = f32[3,4,96,128]{3,2,1,0:T(8,128)S(1)} fusion(f32[3,4,96,128]{3,2,1,0:T(8,128)S(1)} %fusion.30, f32[1,4,96,512]{3,2,1,0:T(8,128)S(1)} %get-tuple-element.10, f32[1,4,96,512]{3,2,1,0:T(8,128)S(1)} %get-tuple-element.9, f32[1,4,96,512]{3,2,1,0:T(8,128)S(1)} %get-tuple-element.8, s32[512]{0:T(512)S(1)} %iota_add_fusion.1, s32[128]{0:T(128)S(1)} %mul.250, ...), kind=kOutput, calls=%fused_computation.30 | convolution fusion | flops 455426048 | bytes 3541632 | tf_op jit(solution)/shard_map/flab,cb->flac/dot_general | solution.py:99
  63.8 0.0 copy-start.4
  63.8 1.9 %fusion.36 = bf16[3,4,96,128]{3,2,1,0:T(8,128)(2,1)S(1)} fusion(f32[3,4,96,128]{3,2,1,0:T(8,128)S(1)} %fusion.27, f32[1,4,96,512]{3,2,1,0:T(8,128)S(1)} %get-tuple-element.7, f32[1,4,96,512]{3,2,1,0:T(8,128)S(1)} %get-tuple-element.6, f32[1,4,96,512]{3,2,1,0:T(8,128)S(1)} %get-tuple-element.5, s32[512]{0:T(512)S(1)} %iota_add_fusion, s32[128]{0:T(128)S(1)} %mul.250, ...), kind=kOutput, calls=%fused_computation.33 | convolution fusion | flops 455720960 | bytes 3246720 | tf_op jit(solution)/shard_map/flab,cb->flac/dot_general | solution.py:99
  65.7 1.0 %copy.81 = bf16[3,4,96,128]{2,1,0,3:T(4,128)(2,1)} copy(bf16[3,4,96,128]{3,2,1,0:T(8,128)(2,1)S(1)} %fusion.36) | data formatting | bytes 589824 | tf_op jit(solution)/shard_map/convert_element_type | solution.py:106
  66.6 5.0 %all-to-all-start.1 = ((bf16[3,4,96,128]{2,1,0,3:T(4,128)(2,1)}), bf16[3,4,96,128]{2,1,0,3:T(4,128)(2,1)S(1)}, u32[]{:S(2)}, u32[]{:S(2)}) async-start(bf16[3,4,96,128]{2,1,0,3:T(4,128)(2,1)} %copy.81), calls=%async_computation.1 | async-start | bytes 786432 | tf_op jit(solution)/shard_map/all_to_all | solution.py:108
  71.6 0.0 copy-done.4
  71.6 0.1 dynamic-slice_bitcast_fusion
  71.7 0.1 slice_bitcast_fusion
  71.8 0.1 slice_bitcast_fusion.1
  71.8 9.2 %all-to-all-done.1 = bf16[3,4,96,128]{2,1,0,3:T(4,128)(2,1)S(1)} async-done(((bf16[3,4,96,128]{2,1,0,3:T(4,128)(2,1)}), bf16[3,4,96,128]{2,1,0,3:T(4,128)(2,1)S(1)}, u32[]{:S(2)}, u32[]{:S(2)}) %all-to-all-start.1) | async-done | bytes 294944 | tf_op jit(solution)/shard_map/all_to_all | solution.py:108
  81.0 0.1 copy.82
  81.1 0.1 convert_bitcast_fusion
  81.2 0.0 copy-start.2
  81.2 0.2 copy.83
  81.4 0.0 copy-start.1
  81.5 0.4 reshape.330
  81.9 0.4 copy.115
  82.3 0.0 copy-done.2
  82.3 0.1 fusion.65
  82.4 0.4 fusion.40
  82.8 0.0 copy-done.1
  82.9 6.2 %collective-permute-start = (bf16[3,2,2,4,65]{4,2,1,0,3:T(2,128)(2,1)S(1)}, bf16[3,2,2,4,65]{4,2,1,0,3:T(2,128)(2,1)S(1)}, u32[]{:S(2)}, u32[]{:S(2)}) collective-permute-start(bf16[3,2,2,4,65]{4,2,1,0,3:T(2,128)(2,1)S(1)} %get-tuple-element.19), channel_id=1, source_target_pairs={{0,1},{1,2},{2,3},{4,5},{5,6},{6,7},{8,9},{9,10},{10,11},{12,13},{... | collective-permute-start | bytes 18728 | tf_op jit(solution)/shard_map/ppermute | solution.py:19
  89.1 1.9 %collective-permute-start.1 = (bf16[3,2,2,4,65]{4,2,1,0,3:T(2,128)(2,1)S(1)}, bf16[3,2,2,4,65]{4,2,1,0,3:T(2,128)(2,1)S(1)}, u32[]{:S(2)}, u32[]{:S(2)}) collective-permute-start(bf16[3,2,2,4,65]{4,2,1,0,3:T(2,128)(2,1)S(1)} %get-tuple-element.20), channel_id=1, source_target_pairs={{1,0},{2,1},{3,2},{5,4},{6,5},{7,6},{9,8},{10,9},{11,10},{13,12},{... | collective-permute-start | bytes 18728 | tf_op jit(solution)/shard_map/ppermute | solution.py:21
  91.0 0.0 collective-permute-done
  91.0 3.1 %collective-permute-done.1 = bf16[3,2,2,4,65]{4,2,1,0,3:T(2,128)(2,1)S(1)} collective-permute-done((bf16[3,2,2,4,65]{4,2,1,0,3:T(2,128)(2,1)S(1)}, bf16[3,2,2,4,65]{4,2,1,0,3:T(2,128)(2,1)S(1)}, u32[]{:S(2)}, u32[]{:S(2)}) %collective-permute-start.1) | collective-permute-done | bytes 6272 | tf_op jit(solution)/shard_map/ppermute | solution.py:21
  94.1 0.1 maximum_convert_fusion
  94.1 0.1 fusion.102
  94.2 0.1 fusion.105
  94.3 0.6 copy.88
  (20 shorter events, 0.2 us)
Async XLA Ops:
  0.0 2.3 %copy-start = (bf16[4,65,384]{2,0,1:T(4,128)(2,1)S(1)}, bf16[4,65,384]{2,0,1:T(4,128)(2,1)}, u32[]{:S(2)}) copy-start(bf16[4,65,384]{2,0,1:T(4,128)(2,1)} %param.8) | copy-start | bytes 599044
  9.1 13.3 %copy-start.5 = (u32[32]{0:T(128)S(1)}, u32[32]{0:T(128)}, u32[]{:S(2)}) copy-start(u32[32]{0:T(128)} %constant.104) | copy-start | bytes 388
  9.1 14.6 %copy-start.3 = (s32[4]{0:T(128)S(1)}, s32[4]{0:T(128)}, u32[]{:S(2)}) copy-start(s32[4]{0:T(128)} %param.9) | copy-start | bytes 52
  16.1 21.7 %all-to-all-start = ((bf16[8,2,18432]{2,1,0:T(2,128)(2,1)}), bf16[8,2,18432]{2,1,0:T(2,128)(2,1)S(1)}, u32[]{:S(2)}, u32[]{:S(2)}) async-start(bf16[8,2,18432]{2,1,0:T(2,128)(2,1)} %reshape.343), calls=%async_computation | async-start | bytes 1179648 | tf_op jit(solution)/shard_map/all_to_all | solution.py:90
  63.8 7.8 %copy-start.4 = (f32[16]{0:T(128)S(1)}, f32[16]{0:T(128)}, u32[]{:S(2)}) copy-start(f32[16]{0:T(128)} %param.11) | copy-start | bytes 196
  66.6 14.4 %all-to-all-start.1 = ((bf16[3,4,96,128]{2,1,0,3:T(4,128)(2,1)}), bf16[3,4,96,128]{2,1,0,3:T(4,128)(2,1)S(1)}, u32[]{:S(2)}, u32[]{:S(2)}) async-start(bf16[3,4,96,128]{2,1,0,3:T(4,128)(2,1)} %copy.81), calls=%async_computation.1 | async-start | bytes 786432 | tf_op jit(solution)/shard_map/all_to_all | solution.py:108
  81.2 1.1 %copy-start.2 = (f32[384]{0:T(512)S(1)}, f32[384]{0:T(512)}, u32[]{:S(2)}) copy-start(f32[384]{0:T(512)} %param.10) | copy-start | bytes 4612
  81.4 1.4 %copy-start.1 = (bf16[3,2,4,4,65]{4,3,2,1,0:T(4,128)(2,1)S(1)}, bf16[3,2,4,4,65]{4,3,2,1,0:T(4,128)(2,1)}, u32[]{:S(2)}) copy-start(bf16[3,2,4,4,65]{4,3,2,1,0:T(4,128)(2,1)} %param.6) | copy-start | bytes 37444
  82.9 8.1 %collective-permute-start = (bf16[3,2,2,4,65]{4,2,1,0,3:T(2,128)(2,1)S(1)}, bf16[3,2,2,4,65]{4,2,1,0,3:T(2,128)(2,1)S(1)}, u32[]{:S(2)}, u32[]{:S(2)}) collective-permute-start(bf16[3,2,2,4,65]{4,2,1,0,3:T(2,128)(2,1)S(1)} %get-tuple-element.19), channel_id=1, source_target_pairs={{0,1},{1,2},{2,3},{4,5},{5,6},{6,7},{8,9},{9,10},{10,11},{12,13},{... | collective-permute-start | bytes 18728 | tf_op jit(solution)/shard_map/ppermute | solution.py:19
  89.1 5.0 %collective-permute-start.1 = (bf16[3,2,2,4,65]{4,2,1,0,3:T(2,128)(2,1)S(1)}, bf16[3,2,2,4,65]{4,2,1,0,3:T(2,128)(2,1)S(1)}, u32[]{:S(2)}, u32[]{:S(2)}) collective-permute-start(bf16[3,2,2,4,65]{4,2,1,0,3:T(2,128)(2,1)S(1)} %get-tuple-element.20), channel_id=1, source_target_pairs={{1,0},{2,1},{3,2},{5,4},{6,5},{7,6},{9,8},{10,9},{11,10},{13,12},{... | collective-permute-start | bytes 18728 | tf_op jit(solution)/shard_map/ppermute | solution.py:21
where the time goes:
time: 95.6 us; the launch traced here: 95 us
  local copies, waits for them, and re-layouts  27.5 us (29%)
  starting transfers between devices  19.5 us (20%)
  matrix products  15.7 us (16%)
  blocking collectives  13.4 us (14%)
  waiting for transfers between devices  12.3 us (13%)
  other arithmetic  5.53 us (6%)
  between operations  1.06 us (1%)
    unnamed x1, blocking collectives  13.4 us
    unnamed x17, local copies, waits for them, and re-layouts  12.3 us
    all_to_all x1, waiting for transfers between devices, local(): lax.all_to_all(lamb_spec, 'ma', split_axis=3, concat_axis=2, tiled=True)  9.2 us
    dot_general x4, matrix products, local(): jnp.einsum('flab,cb->flac', lamb_vector, table_block.astype(jnp.float32),...  7.64 us
    dot_general x4, matrix products, local(): jnp.einsum('flac,cb->flab', spec_block, table_block, preferred_element_ty...  7.44 us
    all_to_all x1, starting transfers between devices, local(): lax.all_to_all(spectral, 'ma', split_axis=2, concat_axis=3, tiled=True)  6.37 us
    ppermute x1, starting transfers between devices, with_halo(): lax.ppermute(tail, axis, [(i, (i + 1) % count) for i in range(ends)])  6.19 us
    convert_element_type x2, local copies, waits for them, and re-layouts, local(): spectral.reshape(6, levels_dev, nlat_all, 4 * pair_count)  6.04 us
  transfers between devices with their start and end apart: 4, of which 2 were waited for; matrix products, arithmetic and copies ran while one was open for 1% of the time, Pallas kernels for 0%

commit v1 on v0

--- a/solution.py
+++ b/solution.py
@@ -105,7 +105,10 @@
         )
     lamb_spec = (accumulated * inv_lon).astype(jnp.bfloat16)
     selector = jnp.transpose(mask_bool.astype(jnp.float32), (1, 0, 2, 3))[:, None, None, None]
-    lamb_block = lax.all_to_all(lamb_spec, "ma", split_axis=3, concat_axis=2, tiled=True)
+    lamb_block = jnp.concatenate(
+        lax.all_to_all(jnp.stack(jnp.split(lamb_spec, lax.axis_size("ma"), axis=3)), "ma", 0, 0),
+        axis=2,
+    )
     item_count = lamb_block.shape[0]
     shaped = lamb_block.astype(jnp.float32).reshape(
         item_count, levels_dev, nlat_all, 2, 2, pair_count

time: 95.6 us -> 102 us (1.067)
  local copies, waits for them, and re-layouts: 27.5 us -> 33.4 us
    unnamed x17 -> x24, local copies, waits for them, and re-layouts: 12.3 us -> 16.7 us
    another operation x0 -> x10, local copies, waits for them, and re-layouts: none -> 2.36 us  [local(): jnp.stack(jnp.split(lamb_spec, lax.axis_size('ma'), axis=3))]
where the time goes in v1:
time: 102 us; the launch traced here: 101 us
  local copies, waits for them, and re-layouts  33.4 us (33%)
  starting transfers between devices  19.4 us (19%)
  matrix products  15.8 us (15%)
  blocking collectives  13.4 us (13%)
  waiting for transfers between devices  12.3 us (12%)
  other arithmetic  5.53 us (5%)
  between operations  1.06 us (1%)
    unnamed x24, local copies, waits for them, and re-layouts  16.7 us
    unnamed x1, blocking collectives  13.4 us
    all_to_all x1, waiting for transfers between devices, local(): lax.all_to_all(jnp.stack(jnp.split(lamb_spec, lax.axis_size('ma'), axis=3...  9.2 us
    dot_general x4, matrix products, local(): jnp.einsum('flab,cb->flac', lamb_vector, table_block.astype(jnp.float32),...  7.65 us
    dot_general x4, matrix products, local(): jnp.einsum('flac,cb->flab', spec_block, table_block, preferred_element_ty...  7.44 us
    all_to_all x1, starting transfers between devices, local(): lax.all_to_all(spectral, 'ma', split_axis=2, concat_axis=3, tiled=True)  6.37 us
    ppermute x1, starting transfers between devices, with_halo(): lax.ppermute(tail, axis, [(i, (i + 1) % count) for i in range(ends)])  6.19 us
    convert_element_type x2, local copies, waits for them, and re-layouts, local(): spectral.reshape(6, levels_dev, nlat_all, 4 * pair_count)  6.03 us
  transfers between devices with their start and end apart: 4, of which 2 were waited for; matrix products, arithmetic and copies ran while one was open for 1% of the time, Pallas kernels for 0%

profile of v1, /device:TPU:1, one launch (start us, length us, event | category | flops | bytes accessed | tf_op | source)
XLA Modules:
  0.0 100.9 jit_solution(16123401072569923614)
XLA Ops:
  0.0 0.7 broadcast_subtract_fusion.1
  0.7 0.7 fusion.112
  1.5 0.8 pad_maximum_fusion
  2.3 0.3 convolution_bitcast_fusion
  2.7 0.1 fusion.42
  2.8 0.1 fusion.43
  2.9 0.2 maximum_bitcast_fusion
  3.0 0.2 copy.76
  3.3 5.8 %copy.77 = bf16[6,4,768,16]{3,1,0,2:T(4,128)(2,1)} copy(bf16[6,4,768,16]{2,1,3,0:T(4,128)(2,1)S(1)} %bitcast.129) | data formatting | bytes 1179648 | tf_op jit(solution)/shard_map/convert_element_type | solution.py:78
  9.1 7.0 %reshape.342 = bf16[8,2,18432]{2,1,0:T(2,128)(2,1)} reshape(bf16[768,6,4,16]{3,2,1,0:T(4,128)(2,1)} %bitcast.126) | data formatting | bytes 1179648
  16.1 6.4 %all-to-all-start = ((bf16[8,2,18432]{2,1,0:T(2,128)(2,1)}), bf16[8,2,18432]{2,1,0:T(2,128)(2,1)S(1)}, u32[]{:S(2)}, u32[]{:S(2)}) async-start(bf16[8,2,18432]{2,1,0:T(2,128)(2,1)} %reshape.342), calls=%async_computation | async-start | bytes 1179648 | tf_op jit(solution)/shard_map/all_to_all | solution.py:90
  22.4 0.6 dynamic-slice
  23.7 0.2 dynamic-update-slice
  23.9 13.4 %all-reduce.1 = s32[32]{0:T(128)S(1)} all-reduce(s32[32]{0:T(128)S(1)} %dynamic-update-slice), channel_id=1, replica_groups=mesh['ma'=8,'row'=4] {'ma'}, use_global_device_ids=true, to_apply=%add.1 | all-reduce | flops 32 | bytes 256
  37.3 0.1 reshape.329
  37.5 0.1 mul.250
  37.6 0.1 eq.67
  37.8 4.5 %reshape.343 = bf16[768,6,4,16]{3,2,1,0:T(4,128)(2,1)} reshape(bf16[8,2,18432]{2,1,0:T(2,128)(2,1)S(1)} %all-to-all-done) | data formatting | bytes 1179648
  42.2 6.0 %copy.113 = bf16[6,4,8,96,16]{3,4,2,1,0:T(8,128)(2,1)S(1)} copy(bf16[6,4,8,96,16]{4,1,0,3,2:T(4,128)(2,1)} %bitcast.127) | data formatting | bytes 1179648 | tf_op jit(solution)/shard_map/all_to_all | solution.py:90
  48.3 1.9 %broadcast_multiply_fusion.3 = f32[6,4,96,512]{3,2,1,0:T(8,128)S(1)} fusion(bf16[6,4,96,128]{2,3,1,0:T(8,128)(2,1)S(1)} %bitcast.122, s32[128]{0:T(128)S(1)} %mul.250, pred[128]{0:T(512)(128)(4,1)S(1)} %eq.67), kind=kOutput, calls=%fused_computation.27 | convolution fusion | flops 304283648 | bytes 5309056 | tf_op jit(solution)/shard_map/flac,cb->flab/dot_general | solution.py:95
  50.1 0.6 multiply_subtract_fusion.11
  50.7 1.9 %broadcast_multiply_fusion.2 = f32[6,4,96,512]{3,2,1,0:T(8,128)S(1)} fusion(bf16[6,4,96,128]{2,3,1,0:T(8,128)(2,1)S(1)} %bitcast.123, s32[512]{0:T(512)S(1)} %iota_add_fusion.2, s32[128]{0:T(128)S(1)} %mul.250, pred[128]{0:T(512)(128)(4,1)S(1)} %eq.67), kind=kOutput, calls=%fused_computation.26 | convolution fusion | flops 304283648 | bytes 5311104 | tf_op jit(solution)/shard_map/flac,cb->flab/dot_general | solution.py:95
  52.6 0.6 multiply_subtract_fusion.8
  53.1 1.9 %broadcast_multiply_fusion.1 = f32[6,4,96,512]{3,2,1,0:T(8,128)S(1)} fusion(bf16[6,4,96,128]{2,3,1,0:T(8,128)(2,1)S(1)} %bitcast.124, s32[512]{0:T(512)S(1)} %iota_add_fusion.1, s32[128]{0:T(128)S(1)} %mul.250, pred[128]{0:T(512)(128)(4,1)S(1)} %eq.67), kind=kOutput, calls=%fused_computation.25 | convolution fusion | flops 304283648 | bytes 5311104 | tf_op jit(solution)/shard_map/flac,cb->flab/dot_general | solution.py:95
  55.0 0.6 multiply_subtract_fusion.5
  55.6 1.9 %broadcast_multiply_fusion = f32[6,4,96,512]{3,2,1,0:T(8,128)S(1)} fusion(bf16[6,4,96,128]{2,3,1,0:T(8,128)(2,1)S(1)} %bitcast.125, s32[512]{0:T(512)S(1)} %iota_add_fusion, s32[128]{0:T(128)S(1)} %mul.250, pred[128]{0:T(512)(128)(4,1)S(1)} %eq.67), kind=kOutput, calls=%fused_computation.24 | convolution fusion | flops 304283648 | bytes 5311104 | tf_op jit(solution)/shard_map/flac,cb->flab/dot_general | solution.py:95
  57.4 0.6 multiply_subtract_fusion.2
  58.0 1.8 %fusion = f32[3,4,96,128]{3,2,1,0:T(8,128)S(1)} fusion(f32[1,4,96,512]{3,2,1,0:T(8,128)S(1)} %get-tuple-element.16, f32[1,4,96,512]{3,2,1,0:T(8,128)S(1)} %get-tuple-element.15, f32[1,4,96,512]{3,2,1,0:T(8,128)S(1)} %get-tuple-element.14, s32[128]{0:T(128)S(1)} %mul.250, pred[128]{0:T(512)(128)(4,1)S(1)} %eq.67), kind=kOutput, calls=%fused_computation | convolution fusion | flops 455278592 | bytes 2949760 | tf_op jit(solution)/shard_map/flab,cb->flac/dot_general | solution.py:99
  59.9 2.1 %fusion.30 = f32[3,4,96,128]{3,2,1,0:T(8,128)S(1)} fusion(f32[3,4,96,128]{3,2,1,0:T(8,128)S(1)} %fusion, f32[1,4,96,512]{3,2,1,0:T(8,128)S(1)} %get-tuple-element.13, f32[1,4,96,512]{3,2,1,0:T(8,128)S(1)} %get-tuple-element.12, f32[1,4,96,512]{3,2,1,0:T(8,128)S(1)} %get-tuple-element.11, s32[512]{0:T(512)S(1)} %iota_add_fusion.2, s32[128]{0:T(128)S(1)} %mul.250, ...), kind=kOutput, calls=%fused_computation.31 | convolution fusion | flops 455426048 | bytes 3541632 | tf_op jit(solution)/shard_map/flab,cb->flac/dot_general | solution.py:99
  61.9 1.9 %fusion.27 = f32[3,4,96,128]{3,2,1,0:T(8,128)S(1)} fusion(f32[3,4,96,128]{3,2,1,0:T(8,128)S(1)} %fusion.30, f32[1,4,96,512]{3,2,1,0:T(8,128)S(1)} %get-tuple-element.10, f32[1,4,96,512]{3,2,1,0:T(8,128)S(1)} %get-tuple-element.9, f32[1,4,96,512]{3,2,1,0:T(8,128)S(1)} %get-tuple-element.8, s32[512]{0:T(512)S(1)} %iota_add_fusion.1, s32[128]{0:T(128)S(1)} %mul.250, ...), kind=kOutput, calls=%fused_computation.30 | convolution fusion | flops 455426048 | bytes 3541632 | tf_op jit(solution)/shard_map/flab,cb->flac/dot_general | solution.py:99
  63.8 1.9 %fusion.36 = bf16[3,4,96,128]{3,2,1,0:T(8,128)(2,1)S(1)} fusion(f32[3,4,96,128]{3,2,1,0:T(8,128)S(1)} %fusion.27, f32[1,4,96,512]{3,2,1,0:T(8,128)S(1)} %get-tuple-element.7, f32[1,4,96,512]{3,2,1,0:T(8,128)S(1)} %get-tuple-element.6, f32[1,4,96,512]{3,2,1,0:T(8,128)S(1)} %get-tuple-element.5, s32[512]{0:T(512)S(1)} %iota_add_fusion, s32[128]{0:T(128)S(1)} %mul.250, ...), kind=kOutput, calls=%fused_computation.33 | convolution fusion | flops 455720960 | bytes 3246720 | tf_op jit(solution)/shard_map/flab,cb->flac/dot_general | solution.py:99
  65.7 0.6 slice_bitcast_fusion
  66.3 0.1 copy.86
  66.5 0.6 constant_dynamic-update-slice_fusion.7
  67.1 0.1 copy.87
  67.2 0.1 copy.88
  67.4 0.1 copy.89
  67.5 0.1 copy.90
  67.7 0.1 copy.91
  67.8 0.1 copy.92
  68.0 0.1 copy.93
  68.1 0.6 constant_dynamic-update-slice_fusion.6
  68.7 0.6 constant_dynamic-update-slice_fusion.5
  69.3 0.6 constant_dynamic-update-slice_fusion.4
  70.0 0.6 constant_dynamic-update-slice_fusion.3
  70.6 0.6 constant_dynamic-update-slice_fusion.2
  71.2 0.6 constant_dynamic-update-slice_fusion.1
  71.8 0.6 constant_dynamic-update-slice_fusion
  72.4 5.0 %all-to-all-start.1 = ((bf16[8,3,4,96,16]{3,4,2,1,0:T(8,128)(2,1)}), bf16[8,3,4,96,16]{3,4,2,1,0:T(8,128)(2,1)S(1)}, u32[]{:S(2)}, u32[]{:S(2)}) async-start(bf16[8,3,4,96,16]{3,4,2,1,0:T(8,128)(2,1)} %constant_dynamic-update-slice_fusion), calls=%async_computation.1 | async-start | bytes 786432 | tf_op jit(solution)/shard_map/all_to_all | solution.py:109
  77.4 0.1 dynamic-slice_bitcast_fusion
  77.5 0.1 slice_bitcast_fusion.8
  77.6 0.1 slice_bitcast_fusion.9
  77.6 9.2 %all-to-all-done.1 = bf16[8,3,4,96,16]{3,4,2,1,0:T(8,128)(2,1)S(1)} async-done(((bf16[8,3,4,96,16]{3,4,2,1,0:T(8,128)(2,1)}), bf16[8,3,4,96,16]{3,4,2,1,0:T(8,128)(2,1)S(1)}, u32[]{:S(2)}, u32[]{:S(2)}) %all-to-all-start.1) | async-done | bytes 294944 | tf_op jit(solution)/shard_map/all_to_all | solution.py:109
  86.9 0.5 copy.94
  87.4 0.4 reshape.330
  87.8 0.4 copy.126
  88.2 0.1 fusion.65
  88.4 0.4 fusion.40
  88.8 6.2 %collective-permute-start = (bf16[3,2,2,4,65]{4,2,1,0,3:T(2,128)(2,1)S(1)}, bf16[3,2,2,4,65]{4,2,1,0,3:T(2,128)(2,1)S(1)}, u32[]{:S(2)}, u32[]{:S(2)}) collective-permute-start(bf16[3,2,2,4,65]{4,2,1,0,3:T(2,128)(2,1)S(1)} %get-tuple-element.27), channel_id=1, source_target_pairs={{0,1},{1,2},{2,3},{4,5},{5,6},{6,7},{8,9},{9,10},{10,11},{12,13},{... | collective-permute-start | bytes 18728 | tf_op jit(solution)/shard_map/ppermute | solution.py:19
  95.0 1.9 %collective-permute-start.1 = (bf16[3,2,2,4,65]{4,2,1,0,3:T(2,128)(2,1)S(1)}, bf16[3,2,2,4,65]{4,2,1,0,3:T(2,128)(2,1)S(1)}, u32[]{:S(2)}, u32[]{:S(2)}) collective-permute-start(bf16[3,2,2,4,65]{4,2,1,0,3:T(2,128)(2,1)S(1)} %get-tuple-element.28), channel_id=1, source_target_pairs={{1,0},{2,1},{3,2},{5,4},{6,5},{7,6},{9,8},{10,9},{11,10},{13,12},{... | collective-permute-start | bytes 18728 | tf_op jit(solution)/shard_map/ppermute | solution.py:21
  97.0 3.1 %collective-permute-done.1 = bf16[3,2,2,4,65]{4,2,1,0,3:T(2,128)(2,1)S(1)} collective-permute-done((bf16[3,2,2,4,65]{4,2,1,0,3:T(2,128)(2,1)S(1)}, bf16[3,2,2,4,65]{4,2,1,0,3:T(2,128)(2,1)S(1)}, u32[]{:S(2)}, u32[]{:S(2)}) %collective-permute-start.1) | collective-permute-done | bytes 6272 | tf_op jit(solution)/shard_map/ppermute | solution.py:21
  100.1 0.1 fusion.102
  100.2 0.1 fusion.105
  100.3 0.6 copy.99
  (35 shorter events, 0.3 us)
Async XLA Ops:
  0.0 2.3 %copy-start = (bf16[4,65,384]{2,0,1:T(4,128)(2,1)S(1)}, bf16[4,65,384]{2,0,1:T(4,128)(2,1)}, u32[]{:S(2)}) copy-start(bf16[4,65,384]{2,0,1:T(4,128)(2,1)} %param.8) | copy-start | bytes 599044
  9.1 13.3 %copy-start.5 = (u32[32]{0:T(128)S(1)}, u32[32]{0:T(128)}, u32[]{:S(2)}) copy-start(u32[32]{0:T(128)} %constant.104) | copy-start | bytes 388
  9.1 14.6 %copy-start.3 = (s32[4]{0:T(128)S(1)}, s32[4]{0:T(128)}, u32[]{:S(2)}) copy-start(s32[4]{0:T(128)} %param.9) | copy-start | bytes 52
  16.1 21.7 %all-to-all-start = ((bf16[8,2,18432]{2,1,0:T(2,128)(2,1)}), bf16[8,2,18432]{2,1,0:T(2,128)(2,1)S(1)}, u32[]{:S(2)}, u32[]{:S(2)}) async-start(bf16[8,2,18432]{2,1,0:T(2,128)(2,1)} %reshape.342), calls=%async_computation | async-start | bytes 1179648 | tf_op jit(solution)/shard_map/all_to_all | solution.py:90
  66.3 11.1 %copy-start.4 = (f32[16]{0:T(128)S(1)}, f32[16]{0:T(128)}, u32[]{:S(2)}) copy-start(f32[16]{0:T(128)} %param.11) | copy-start | bytes 196
  72.4 14.4 %all-to-all-start.1 = ((bf16[8,3,4,96,16]{3,4,2,1,0:T(8,128)(2,1)}), bf16[8,3,4,96,16]{3,4,2,1,0:T(8,128)(2,1)S(1)}, u32[]{:S(2)}, u32[]{:S(2)}) async-start(bf16[8,3,4,96,16]{3,4,2,1,0:T(8,128)(2,1)} %constant_dynamic-update-slice_fusion), calls=%async_computation.1 | async-start | bytes 786432 | tf_op jit(solution)/shard_map/all_to_all | solution.py:109
  86.9 1.3 %copy-start.2 = (f32[384]{0:T(512)S(1)}, f32[384]{0:T(512)}, u32[]{:S(2)}) copy-start(f32[384]{0:T(512)} %param.10) | copy-start | bytes 4612
  87.4 1.4 %copy-start.1 = (bf16[3,2,4,4,65]{4,3,2,1,0:T(4,128)(2,1)S(1)}, bf16[3,2,4,4,65]{4,3,2,1,0:T(4,128)(2,1)}, u32[]{:S(2)}) copy-start(bf16[3,2,4,4,65]{4,3,2,1,0:T(4,128)(2,1)} %param.6) | copy-start | bytes 37444
  88.8 8.1 %collective-permute-start = (bf16[3,2,2,4,65]{4,2,1,0,3:T(2,128)(2,1)S(1)}, bf16[3,2,2,4,65]{4,2,1,0,3:T(2,128)(2,1)S(1)}, u32[]{:S(2)}, u32[]{:S(2)}) collective-permute-start(bf16[3,2,2,4,65]{4,2,1,0,3:T(2,128)(2,1)S(1)} %get-tuple-element.27), channel_id=1, source_target_pairs={{0,1},{1,2},{2,3},{4,5},{5,6},{6,7},{8,9},{9,10},{10,11},{12,13},{... | collective-permute-start | bytes 18728 | tf_op jit(solution)/shard_map/ppermute | solution.py:19
  95.0 5.0 %collective-permute-start.1 = (bf16[3,2,2,4,65]{4,2,1,0,3:T(2,128)(2,1)S(1)}, bf16[3,2,2,4,65]{4,2,1,0,3:T(2,128)(2,1)S(1)}, u32[]{:S(2)}, u32[]{:S(2)}) collective-permute-start(bf16[3,2,2,4,65]{4,2,1,0,3:T(2,128)(2,1)S(1)} %get-tuple-element.28), channel_id=1, source_target_pairs={{1,0},{2,1},{3,2},{5,4},{6,5},{7,6},{9,8},{10,9},{11,10},{13,12},{... | collective-permute-start | bytes 18728 | tf_op jit(solution)/shard_map/ppermute | solution.py:21
